TPU v7x, 128 devices: a whole 4x4x4 slice. The times are simulated.
128 devices in a mesh: seq: 16 (over x, z), head: 8 (over y, core).
Axes of the slice: x: 4, y: 4, z: 4, core: 2. Of those that a mesh axis runs over, the one named last changes fastest.
Arguments:
- tokens: bfloat16 [2048, 4, 2048], P('seq', None, 'head'), may hold values from -6 to 6
- attn_gain: bfloat16 [2048], replicated, may hold values from 0.25 to 1.75
- query_weight: bfloat16 [2048, 2048], P(None, 'head'), may hold values from -0.125 to 0.125
- key_weight: bfloat16 [2048, 2048], P(None, 'head'), may hold values from -0.125 to 0.125
- value_weight: bfloat16 [2048, 2048], P(None, 'head'), may hold values from -0.125 to 0.125
- head_gain: bfloat16 [2048], P('head'), may hold values from 0.25 to 1.75
- out_weight: bfloat16 [2048, 2048], P('head'), may hold values from -0.125 to 0.125
- moe_gain: bfloat16 [2048], replicated, may hold values from 0.25 to 1.75
- route_ids: int32 [2048, 4, 8], P(('seq', 'head')), may hold values from 0 to 63, all different within a row; in each aligned block of 64 rows (0 to 63, 64 to 127, ..., all dimensions but the last counted through in order) at most 12 rows name the same one
- route_weight: float32 [2048, 4, 8], P(('seq', 'head')), may hold values from 0.05 to 0.3
- expert_gate: bfloat16 [128, 2048, 512], P(('seq', 'head')), may hold values from -0.125 to 0.125
- expert_up: bfloat16 [128, 2048, 512], P(('seq', 'head')), may hold values from -0.125 to 0.125
- expert_down: bfloat16 [128, 512, 2048], P(('seq', 'head')), may hold values from -0.1875 to 0.1875
Outputs:
- layer_output: bfloat16 [2048, 4, 2048], P(('seq', 'head'))
Inputs may be any that keep to these rules, and one draw needn't show every extreme that they name: `route_ids`: the rows [position, sequence] taken position-major form aligned blocks of 64 rows, the rows of one device; within every block no expert is named by more than 12 routes, and in every draw some block has an expert named by exactly 12 routes. The 8 experts of a row differ.
All inputs are finite; a program needn't handle non-finite values.
Results may differ from a plain program's by a relative error of at most 0.017.
Values may be sent and summed in bfloat16 or wider, within the bound.
No kernel may reach another device: no remote copies, remote signals or barrier semaphores. Data moves between devices by JAX's collectives and lax.ppermute only.
A program may use at most 128 MiB of HBM per device.

v0:
```python
import jax
import jax.numpy as jnp
import numpy as np
from jax import lax
from jax.experimental import pallas as pl
from jax.experimental.pallas import tpu as pltpu
from jax.sharding import Mesh, PartitionSpec as P


EXPERTS = 64
TOP = 8
CAP = 12
QUART = 4
PACK = CAP * QUART
COLS = EXPERTS * PACK
WIDE = 8
REST = CAP - WIDE
GROUP = 16
EARLY = (0, 1, 2, 4)

norm_eps = 1e-05
head_eps = 1e-06

BF = jnp.bfloat16
F32 = jnp.float32


def shifted(x, axis, by):
    count = lax.axis_size(axis)
    return lax.ppermute(x, axis, [(i, (i + by) % count) for i in range(count)])


def swirled(x, by):
    ways = lax.axis_size("y")
    pairs = [(2 * y + c, 2 * ((y + (by if c == 0 else -by)) % ways) + c) for y in range(ways) for c in range(2)]
    return lax.ppermute(x, ("y", "c"), pairs)


def exchanged(x, axes):
    return lax.all_to_all(x, axes, split_axis=0, concat_axis=0, tiled=True)


def dot(a, b, dims=((1,), (0,))):
    return lax.dot_general(a, b, (dims, ((), ())), preferred_element_type=F32)


def silu(v):
    return v / (1.0 + jnp.exp(-v))


INSIDE = pl.BlockSpec(memory_space=pltpu.VMEM)
OUTSIDE = pl.BlockSpec(memory_space=pltpu.HBM)


class Placed:
    def __init__(self, x, spec, fixed):
        self.x = x if fixed is None else pltpu.with_memory_space_constraint(x, fixed)
        self.spec = spec


def inside(x):
    return Placed(x, INSIDE, pltpu.VMEM)


def outside(x):
    return Placed(x, OUTSIDE, pltpu.HBM)


def loaded(x):
    return Placed(x, INSIDE, pltpu.HBM)


def either(x):
    return Placed(x, INSIDE, None)


def call(kernel, out_shape, *args, out_specs=INSIDE, scratch=(), mib=24):
    args = [x if isinstance(x, Placed) else loaded(x) for x in args]
    if isinstance(out_shape, (list, tuple)) and not isinstance(out_specs, (list, tuple)):
        out_specs = [out_specs] * len(out_shape)
    return pl.pallas_call(
        kernel,
        out_shape=out_shape,
        in_specs=[x.spec for x in args],
        out_specs=out_specs,
        scratch_shapes=list(scratch),
        compiler_params=pltpu.CompilerParams(vmem_limit_bytes=mib * 2**20),
    )(*[x.x for x in args])


def route_kernel(ids_ref, weight_ref, *refs):
    given, (send_ref, sum_ref), taken, sem = refs[:4], refs[4:6], refs[6:10], refs[10]
    copies = [copied(source, target, sem.at[i]) for i, (source, target) in enumerate(zip(given, taken))]
    batch, _, span = ids_ref.shape
    rows = batch * span
    ids = jnp.zeros((rows, TOP), F32)
    ids_t = jnp.zeros((TOP, rows), F32)
    weights = jnp.zeros((rows, TOP), F32)
    for b in range(batch):
        row = lax.broadcasted_iota(jnp.int32, (span, rows), 1)
        pick = jnp.where(lax.broadcasted_iota(jnp.int32, (span, rows), 0) * batch + b == row, 1.0, 0.0).astype(BF)
        some = ids_ref[b].astype(F32).astype(BF)
        ids = ids + dot(pick, some, ((0,), (1,)))
        ids_t = ids_t + dot(some, pick)
        weights = weights + dot(pick, weight_ref[b].astype(BF), ((0,), (1,)))
    across = lax.broadcasted_iota(jnp.int32, (rows, EXPERTS), 1).astype(F32)
    down = lax.broadcasted_iota(jnp.int32, (EXPERTS, rows), 0).astype(F32)
    named = jnp.zeros((rows, EXPERTS), F32)
    named_t = jnp.zeros((EXPERTS, rows), F32)
    weight = jnp.zeros((rows, EXPERTS), F32)
    for j in range(TOP):
        hit = ids[:, j : j + 1] == across
        named = named + jnp.where(hit, 1.0, 0.0)
        weight = weight + jnp.where(hit, weights[:, j : j + 1], 0.0)
        named_t = named_t + jnp.where(ids_t[j : j + 1, :] == down, 1.0, 0.0)
    i0 = lax.broadcasted_iota(jnp.int32, (rows, rows), 0)
    i1 = lax.broadcasted_iota(jnp.int32, (rows, rows), 1)
    before = dot(jnp.where(i1 < i0, 1.0, 0.0).astype(BF), named.astype(BF))
    before_t = dot(named_t.astype(BF), jnp.where(i0 < i1, 1.0, 0.0).astype(BF))
    slot = jnp.where(named > 0.5, before, 128.0)
    slot_t = jnp.where(named_t > 0.5, before_t, 128.0)

    def placed(slots, q):
        return jnp.where(slots < WIDE - 0.5, slots + float(WIDE * q), slots + float(WIDE * (QUART - 1) + REST * q))

    slot_all = jnp.concatenate([placed(slot, q) for q in range(QUART)], axis=0).astype(BF)
    slot_all_t = jnp.concatenate([placed(slot_t, q) for q in range(QUART)], axis=1).astype(BF)

    def split(shape, dim, other):
        index = lax.broadcasted_iota(jnp.int32, shape, dim).astype(F32)
        expert = jnp.floor((index + 0.5) * (1.0 / PACK))
        spread = jnp.where(expert == lax.broadcasted_iota(jnp.int32, shape, other).astype(F32), 1.0, 0.0)
        return spread.astype(BF), index - expert * PACK

    spread_t, place_t = split((COLS, EXPERTS), 0, 1)
    send_ref[...] = jnp.where(dot(spread_t, slot_all_t) == place_t[:, :1], 1.0, 0.0).astype(BF)
    spread, place = split((EXPERTS, COLS), 1, 0)
    match = dot(slot_all, spread) == place[:1, :]
    weight_all = dot(weight.astype(BF), spread)
    sum_ref[...] = jnp.where(match, jnp.concatenate([weight_all] * QUART, axis=0), 0.0).astype(BF)
    wait_all(copies)


def copied(source, target, sem):
    copy = pltpu.make_async_copy(source, target, sem)
    copy.start()
    return copy


def wait_all(copies):
    for copy in copies:
        copy.wait()


def block_order():
    y = lax.axis_index("y")
    c = lax.axis_index("c")
    return [((y + away) & 3) * 2 + core for core in (c, 1 - c) for away in (0, 3 - 2 * core, 1 + 2 * core, 2)]


def products(pieces, blocks, weight_refs, gain_ref, scaled_ref, rows_ref):
    rows, width = pieces[0].shape
    total = jnp.zeros((rows, 1), F32)
    for i, (ref, block) in enumerate(zip(pieces, blocks)):
        values = ref[...].astype(F32)
        total = total + jnp.sum(values * values, axis=1, keepdims=True)
        gain = jnp.concatenate([gain_ref[pl.ds(2 * block + j, 1), :] for j in range(2)], axis=1)
        scaled_ref[:, i * width : (i + 1) * width] = (values * gain).astype(BF)
    out = []
    for w, ref in enumerate(weight_refs):
        for i, block in enumerate(blocks):
            start = pl.multiple_of(block * width, width)
            rows_ref[w, i * width : (i + 1) * width, :] = ref[pl.ds(start, width), :]
        out.append(dot(scaled_ref[...], rows_ref[w]))
    return total, out


def early_kernel(*refs):
    pieces, weights = refs[:4], refs[4:7]
    gain_ref, total_ref, sum_ref, gain_rows_ref, scaled_ref, rows_ref = refs[7:]
    gain_rows_ref[...] = gain_ref[...].astype(F32)
    blocks = block_order()
    total, out = products(pieces, [blocks[i] for i in EARLY], weights, gain_rows_ref, scaled_ref, rows_ref)
    total_ref[...] = jnp.broadcast_to(total, total_ref.shape)
    for w in range(3):
        sum_ref[w] = out[w]


def local_kernel(*refs):
    pieces, weights, refs = refs[:8], refs[8:11], refs[11:]
    gain_ref, total_ref, sum_ref, q_ref, local_ref, state_ref, own_ref, gain_rows_ref, scaled_ref, rows_ref = refs
    gain_rows_ref[...] = gain_ref[...].astype(F32)
    rows, width = pieces[0].shape
    blocks = block_order()
    late = [i for i in range(8) if i not in EARLY]
    total, out = products(
        [pieces[i] for i in late], [blocks[i] for i in late], weights, gain_rows_ref, scaled_ref, rows_ref
    )
    scale = lax.rsqrt((total + total_ref[:, :1]) / (8 * width) + norm_eps)
    own_rows = rows // 8
    start = pl.multiple_of((lax.axis_index("y") * 2 + lax.axis_index("c")) * own_rows, own_rows)
    for ref, block in zip(pieces, blocks):
        own_ref[:, pl.ds(pl.multiple_of(block * width, width), width)] = ref[pl.ds(start, own_rows), :]
    k = silu((out[0] + sum_ref[0]) * scale).astype(BF)
    v = ((out[1] + sum_ref[1]) * scale).astype(BF)
    q = silu((out[2] + sum_ref[2]) * scale).astype(BF)
    q_ref[...] = q
    i0 = lax.broadcasted_iota(jnp.int32, (rows, rows), 0)
    i1 = lax.broadcasted_iota(jnp.int32, (rows, rows), 1)
    seen = (((i0 ^ i1) & 3) == 0) & (i1 <= i0)
    sequence = lax.broadcasted_iota(jnp.int32, (rows, 128), 0) & 3
    for h in range(2):
        cols = slice(h * 128, (h + 1) * 128)
        keys = k[:, cols].astype(F32)
        apart = jnp.concatenate([jnp.where(sequence == b, keys, 0.0).astype(BF) for b in range(4)], axis=1)
        state_ref[h * rows : (h + 1) * rows, :] = dot(apart, v[:, cols], ((0,), (0,))).astype(BF)
        scores = jnp.where(seen, dot(q[:, cols], k[:, cols], ((1,), (1,))), 0.0).astype(BF)
        local_ref[:, cols] = dot(scores, v[:, cols])


def prefix_kernel(states_ref, before_ref):
    running = jnp.zeros(states_ref.shape[1:], F32)
    for i in range(states_ref.shape[0]):
        before_ref[i] = running.astype(BF)
        running = running + states_ref[i].astype(F32)


def mix_kernel(q_ref, local_ref, carried_ref, gain_ref, out_ref):
    rows = q_ref.shape[0]
    sequence = lax.broadcasted_iota(jnp.int32, (rows, 128), 0) & 3
    for h in range(2):
        cols = slice(h * 128, (h + 1) * 128)
        q = q_ref[:, cols].astype(F32)
        apart = jnp.concatenate([jnp.where(sequence == b, q, 0.0).astype(BF) for b in range(4)], axis=1)
        mixed = local_ref[:, cols] + dot(apart, carried_ref[h * rows : (h + 1) * rows, :])
        mean = jnp.mean(mixed * mixed, axis=1, keepdims=True)
        out_ref[:, cols] = (mixed * lax.rsqrt(mean + head_eps) * gain_ref[h : h + 1, :].astype(F32)).astype(BF)


def dispatch_kernel(*refs):
    weights, refs = refs[:8], refs[8:]
    attended_ref, own_ref, gain_ref, table_ref, residual_ref, out_ref = refs
    _, width = own_ref.shape
    residual = own_ref[...].astype(F32)
    for ref, block in zip(weights, block_order()):
        residual = residual + dot(attended_ref[block], ref[...]).astype(BF).astype(F32)
    residual_ref[...] = residual
    mean = jnp.mean(residual * residual, axis=1, keepdims=True)
    gain = gain_ref[...].astype(F32)
    gain = jnp.concatenate([gain[i : i + 1, :] for i in range(gain.shape[0])], axis=1)
    entering = (residual * lax.rsqrt(mean + norm_eps) * gain).astype(BF)
    step = width // QUART
    stacked = jnp.concatenate([entering[:, q * step : (q + 1) * step] for q in range(QUART)], axis=0)
    out_ref[...] = dot(table_ref[...], stacked).astype(BF)


def expert_kernel(
    rows_ref, order_ref, back_ref, gate_ref, up_ref, down_ref, gate_b_ref, up_b_ref, down_b_ref, out_ref, x_ref
):
    sources, _, step = rows_ref.shape
    head = sources * WIDE
    part = GROUP * REST
    wide = WIDE * QUART
    for q in range(QUART):
        for i in range(sources):
            x_ref[i * WIDE : (i + 1) * WIDE, q * step : (q + 1) * step] = rows_ref[i, q * WIDE : (q + 1) * WIDE, :]
    for g in range(sources // GROUP):
        rest = rows_ref[g * GROUP : (g + 1) * GROUP, wide:, :].reshape(GROUP * REST * QUART, step)
        rest = dot(order_ref[...], rest).astype(BF)
        for q in range(QUART):
            at = head + g * part
            x_ref[at : at + part, q * step : (q + 1) * step] = rest[q * part : (q + 1) * part]
    for lines in (slice(0, head), slice(head, sources * CAP)):
        halves = []
        for gate, up, down in ((gate_ref, up_ref, down_ref), (gate_b_ref, up_b_ref, down_b_ref)):
            gated = dot(x_ref[lines, :], gate[...])
            active = (silu(gated) * dot(x_ref[lines, :], up[...])).astype(BF)
            halves.append(dot(active, down[...]).astype(BF))
        x_ref[lines, :] = (halves[0].astype(F32) + halves[1].astype(F32)).astype(BF)
    for q in range(QUART):
        for i in range(sources):
            out_ref[i, q * WIDE : (q + 1) * WIDE, :] = x_ref[i * WIDE : (i + 1) * WIDE, q * step : (q + 1) * step]
    for g in range(sources // GROUP):
        at = head + g * part
        rest = jnp.concatenate([x_ref[at : at + part, q * step : (q + 1) * step] for q in range(QUART)], axis=0)
        rest = dot(back_ref[...], rest).astype(BF)
        out_ref[g * GROUP : (g + 1) * GROUP, wide:, :] = rest.reshape(GROUP, REST * QUART, step)


def combine_kernel(rows_ref, table_ref, residual_ref, out_ref):
    rows = residual_ref.shape[0]
    step = rows_ref.shape[1]
    total = dot(table_ref[...], rows_ref[...])
    batch = out_ref.shape[1]
    for q in range(QUART):
        cols = slice(q * step, (q + 1) * step)
        out = residual_ref[:, cols] + total[q * rows : (q + 1) * rows]
        for i in range(rows // batch):
            out_ref[i, :, cols] = out[i * batch : (i + 1) * batch].astype(BF)


def sorting():
    size = GROUP * REST * QUART
    order = np.zeros((size, size), np.float32)
    for q in range(QUART):
        for s in range(GROUP):
            for r in range(REST):
                order[(q * GROUP + s) * REST + r, (s * QUART + q) * REST + r] = 1.0
    return order


def body(
    tokens, attn_gain, query_weight, key_weight, value_weight, head_gain, out_weight, moe_gain,
    route_ids, route_weight, expert_gate, expert_up, expert_down,
):
    shape = jax.ShapeDtypeStruct
    block_len, batch, width = tokens.shape
    rows = block_len * batch
    model = attn_gain.shape[0]
    own_rows = rows // 8
    hidden = expert_gate.shape[2]
    order = sorting()

    attn_rows = attn_gain.reshape(-1, 128)
    head_rows = head_gain.reshape(-1, 128)
    moe_rows = moe_gain.reshape(-1, 128)
    mine = tokens.reshape(rows, width)
    first = swirled(mine, 1)
    second = swirled(mine, -1)
    far = swirled(first, 1)
    pieces = [mine, first, second, far]
    pieces = pieces + [shifted(mine, "c", 1)]
    pieces = pieces + [shifted(p, "c", 1) for p in (first, second)]
    pieces = pieces + [shifted(far, "c", 1)]

    out_first = swirled(out_weight, 1)
    out_second = swirled(out_weight, -1)
    out_far = swirled(out_first, 1)
    projections = [None, out_first, out_second, out_far]
    out_other = shifted(out_weight, "c", 1)
    projections = projections + [out_other, shifted(out_first, "c", 1)]
    projections.append(shifted(out_second, "c", 1))
    projections.append(shifted(out_far, "c", 1))
    gate = expert_gate.reshape(model, hidden)
    up = expert_up.reshape(model, hidden)
    down = expert_down.reshape(hidden, model)
    other_gate = shifted(gate, "c", 1)
    other_up = shifted(up, "c", 1)
    other_down = shifted(down, "c", 1)

    early_weights = (key_weight, value_weight, query_weight, out_weight)
    send_table, sum_table, *near_weights = call(
        route_kernel,
        [
            pltpu.VMEM((COLS, QUART * own_rows), BF),
            pltpu.HBM((QUART * own_rows, COLS), BF),
            *[pltpu.VMEM(w.shape, BF) for w in early_weights],
        ],
        route_ids.transpose(1, 2, 0),
        route_weight.transpose(1, 2, 0),
        *[outside(w) for w in early_weights],
        scratch=[pltpu.SemaphoreType.DMA((4,))],
        mib=12,
    )
    projections[0] = near_weights[3]
    scratch = [
        pltpu.VMEM(attn_rows.shape, F32),
        pltpu.VMEM((rows, model // 2), BF),
        pltpu.VMEM((3, model // 2, width), BF),
    ]
    early_total, early_sum = call(
        early_kernel,
        [pltpu.VMEM((rows, 128), F32), pltpu.VMEM((3, rows, width), F32)],
        *[inside(pieces[i]) for i in EARLY],
        *[inside(w) for w in near_weights[:3]],
        attn_rows,
        scratch=scratch,
        mib=16,
    )
    q, local_mix, state, own = call(
        local_kernel,
        (
            pltpu.VMEM((rows, width), BF),
            pltpu.VMEM((rows, width), F32),
            pltpu.VMEM((2 * rows, 128), BF),
            pltpu.VMEM((own_rows, model), BF),
        ),
        *[inside(p) for p in pieces],
        *[inside(w) for w in near_weights[:3]],
        attn_rows,
        inside(early_total),
        inside(early_sum),
        scratch=scratch,
        mib=20,
    )
    blocks = lax.axis_size(("x", "z"))
    states = inside(exchanged(state.reshape(blocks, 2 * rows // blocks, 128), ("x", "z")))
    before = call(prefix_kernel, pltpu.VMEM(states.x.shape, BF), states)
    carried = inside(exchanged(before, ("x", "z")).reshape(2 * rows, 128))
    attended = call(mix_kernel, pltpu.VMEM((rows, width), BF), inside(q), inside(local_mix), carried, head_rows)
    attended = inside(exchanged(attended.reshape(8, own_rows, width), ("y", "c")))
    step = model // QUART
    residual, sending = call(
        dispatch_kernel,
        (pltpu.HBM((own_rows, model), F32), pltpu.VMEM((COLS, step), BF)),
        *[inside(p) for p in projections],
        attended,
        inside(own),
        moe_rows,
        inside(send_table),
    )
    chips = ("x", "z", "y")
    received = inside(exchanged(sending.reshape(EXPERTS, PACK, step), chips))
    results = call(
        expert_kernel,
        pltpu.VMEM((EXPERTS, PACK, step), BF),
        received,
        either(jnp.asarray(order, BF)),
        either(jnp.asarray(order.T, BF)),
        *[inside(w) for w in (gate, up, down, other_gate, other_up, other_down)],
        scratch=[pltpu.VMEM((EXPERTS * CAP, model), BF)],
        mib=20,
    )
    returned = inside(exchanged(results, chips).reshape(COLS, step))
    out = call(combine_kernel, shape((own_rows // batch, batch, model), BF), returned, either(sum_table), either(residual))
    return out


def solution(mesh):
    fine = Mesh(mesh.devices.reshape(4, 4, 4, 2), ("x", "z", "y", "c"))
    seq, head, every = ("x", "z"), ("y", "c"), ("x", "z", "y", "c")
    in_specs = (
        P(seq, None, head),
        P(),
        P(None, head),
        P(None, head),
        P(None, head),
        P(head),
        P(head, None),
        P(),
        P(every, None, None),
        P(every, None, None),
        P(every, None, None),
        P(every, None, None),
        P(every, None, None),
    )

    return jax.shard_map(body, mesh=fine, in_specs=in_specs, out_specs=P(every, None, None), check_vma=False)
```

profile of v0, /device:TPU:1, one launch (start us, length us, event | category | flops | bytes accessed | tf_op | source)
XLA Modules:
  0.0 233.8 jit_solution(11906408994317911474)
XLA Ops:
  0.0 3.6 %collective-permute-start = (bf16[256,2048]{1,0:T(8,128)(2,1)}, bf16[256,2048]{1,0:T(8,128)(2,1)S(1)}, u32[]{:S(2)}, u32[]{:S(2)}) collective-permute-start(bf16[256,2048]{1,0:T(8,128)(2,1)} %refs_3_.1), channel_id=1, source_target_pairs={{0,2},{1,7},{2,4},{3,1},{4,6},{5,3},{6,0},{7,5},{8,10},{9,15},{10,... | collective-permute-start | bytes 3145736 | tf_op jit(solution)/shard_map/ppermute | solution.py:36
  3.6 22.0 %collective-permute-done.refs_1_ = bf16[256,2048]{1,0:T(8,128)(2,1)S(1)} collective-permute-done((bf16[256,2048]{1,0:T(8,128)(2,1)}, bf16[256,2048]{1,0:T(8,128)(2,1)S(1)}, u32[]{:S(2)}, u32[]{:S(2)}) %collective-permute-start) | collective-permute-done | bytes 1048608 | tf_op jit(solution)/shard_map/ppermute | solution.py:36
  25.6 3.4 %collective-permute-start.2 = (bf16[256,2048]{1,0:T(8,128)(2,1)S(1)}, bf16[256,2048]{1,0:T(8,128)(2,1)}, u32[]{:S(2)}, u32[]{:S(2)}) collective-permute-start(bf16[256,2048]{1,0:T(8,128)(2,1)S(1)} %collective-permute-done.refs_1_), channel_id=1, source_target_pairs={{0,2},{1,7},{2,4},{3,1},{4,6},{5,3},{6,0},{7,5},{8,10},{9,15},{10,... | collective-permute-start | bytes 3145736 | tf_op jit(solution)/shard_map/ppermute | solution.py:36
  29.0 1.0 reshape.36.refs_0_
  30.0 0.1 collective-permute-start.7
  30.1 1.5 collective-permute-start.8
  31.6 1.7 collective-permute-start.10
  33.3 13.1 %collective-permute-done.7.refs_1_ = bf16[512,256]{1,0:T(8,128)(2,1)S(1)} collective-permute-done((bf16[512,256]{1,0:T(8,128)(2,1)S(1)}, bf16[512,256]{1,0:T(8,128)(2,1)S(1)}, u32[]{:S(2)}, u32[]{:S(2)}) %collective-permute-start.7) | collective-permute-done | bytes 262176 | tf_op jit(solution)/shard_map/ppermute | solution.py:36
  46.4 3.1 %collective-permute-start.9 = (bf16[512,256]{1,0:T(8,128)(2,1)S(1)}, bf16[512,256]{1,0:T(8,128)(2,1)S(1)}, u32[]{:S(2)}, u32[]{:S(2)}) collective-permute-start(bf16[512,256]{1,0:T(8,128)(2,1)S(1)} %collective-permute-done.7.refs_1_), channel_id=1, source_target_pairs={{0,2},{1,7},{2,4},{3,1},{4,6},{5,3},{6,0},{7,5},{8,10},{9,15},{10,... | collective-permute-start | bytes 786440 | tf_op jit(solution)/shard_map/ppermute | solution.py:36
  49.5 0.5 collective-permute-start.12
  50.0 2.8 %collective-permute-done.9.refs_3_ = bf16[512,256]{1,0:T(8,128)(2,1)S(1)} collective-permute-done((bf16[512,256]{1,0:T(8,128)(2,1)S(1)}, bf16[512,256]{1,0:T(8,128)(2,1)S(1)}, u32[]{:S(2)}, u32[]{:S(2)}) %collective-permute-start.9) | collective-permute-done | bytes 262176 | tf_op jit(solution)/shard_map/ppermute | solution.py:36
  52.8 3.5 %collective-permute-start.3 = (bf16[256,2048]{1,0:T(8,128)(2,1)}, bf16[256,2048]{1,0:T(8,128)(2,1)}, u32[]{:S(2)}, u32[]{:S(2)}) collective-permute-start(bf16[256,2048]{1,0:T(8,128)(2,1)} %refs_3_.1), channel_id=1, source_target_pairs={{0,1},{1,0},{2,3},{3,2},{4,5},{5,4},{6,7},{7,6},{8,9},{9,8},{10,11... | collective-permute-start | bytes 3145736 | tf_op jit(solution)/shard_map/ppermute | solution.py:30
  56.3 0.0 collective-permute-start.4
  56.3 0.5 collective-permute-start.5
  56.9 0.1 collective-permute-start.6
  56.9 0.4 collective-permute-start.13
  57.4 4.1 %shard_map.145 = (bf16[3072,256]{1,0:T(8,128)(2,1)S(1)}, bf16[256,3072]{1,0:T(8,128)(2,1)}, bf16[2048,256]{1,0:T(8,128)(2,1)S(1)}, bf16[2048,256]{1,0:T(8,128)(2...) custom-call(s32[4,8,16]{2,1,0:T(8,128)} %bitcast.23, f32[4,8,16]{2,1,0:T(8,128)} %bitcast.24, ...), custom_call_target="tpu_custom_call" | custom-call | tf_op jit(solution)/shard_map/pallas_call | solution.py:81
  61.5 1.0 copy-done.11
  62.4 1.7 shard_map.146
  64.1 2.8 %shard_map.147 = (bf16[512,256]{1,0:T(8,128)(2,1)S(1)}, f32[512,256]{1,0:T(8,128)S(1)}, bf16[1024,128]{1,0:T(8,128)(2,1)S(1)}, bf16[64,2048]{1,0:T(8,128)(2,1)S(1)}) custom-call(bf16[512,256]{1,0:T(8,128)(2,1)S(1)} %reshape.36.refs_0_, bf16[512,256]{1,0:T(8,128)(2,1)S(1)} %collective-permute-done.7.refs_1_, ...), custom_call_target="tpu_custom_call" | custom-call | tf_op jit(solution)/shard_map/pallas_call | solution.py:81
  66.9 15.4 %all_to_all.25.states_ref = bf16[16,64,128]{2,1,0:T(8,128)(2,1)S(1)} all-to-all(bf16[16,64,128]{2,1,0:T(8,128)(2,1)S(1)} %bitcast.22), channel_id=1, replica_groups=mesh['x'=4,'z'=4,'y'=4,'c'=2] {'x','z'}, dimensions={0} | all-to-all | bytes 524288 | tf_op jit(solution)/shard_map/all_to_all | solution.py:40
  82.3 11.0 %all_to_all.26 = bf16[16,64,128]{2,1,0:T(8,128)(2,1)S(1)} all-to-all(bf16[16,64,128]{2,1,0:T(8,128)(2,1)S(1)} %shard_map.148), channel_id=1, replica_groups=mesh['x'=4,'z'=4,'y'=4,'c'=2] {'x','z'}, dimensions={0} | all-to-all | bytes 524288 | tf_op jit(solution)/shard_map/all_to_all | solution.py:40
  93.3 1.9 shard_map.149
  95.2 6.0 %all-to-all-start.2 = ((bf16[8,64,256]{2,1,0:T(8,128)(2,1)}), bf16[8,64,256]{2,1,0:T(8,128)(2,1)S(1)}, u32[]{:S(2)}, u32[]{:S(2)}) async-start(bf16[8,64,256]{2,1,0:T(8,128)(2,1)} %bitcast.6), calls=%async_computation.2 | async-start | bytes 524288 | tf_op jit(solution)/shard_map/all_to_all | solution.py:40
  101.2 6.5 %all-to-all-done.2.refs_8_ = bf16[8,64,256]{2,1,0:T(8,128)(2,1)S(1)} async-done(((bf16[8,64,256]{2,1,0:T(8,128)(2,1)}), bf16[8,64,256]{2,1,0:T(8,128)(2,1)S(1)}, u32[]{:S(2)}, u32[]{:S(2)}) %all-to-all-start.2) | async-done | bytes 262176 | tf_op jit(solution)/shard_map/all_to_all | solution.py:40
  107.7 1.2 copy-done.12
  108.9 5.5 %shard_map.150 = (f32[64,2048]{1,0:T(8,128)}, bf16[3072,512]{1,0:T(8,128)(2,1)S(1)}) custom-call(bf16[256,2048]{1,0:T(8,128)(2,1)S(1)} %copy-done.12, bf16[256,2048]{1,0:T(8,128)(2,1)S(1)} %collective-permute-done.refs_1_, bf16[256,2048]{1,0:T(8,128)(2,1)} %collective-permute-done.1.refs_2_, bf16[256,2048]{1,0:T(8,128)(2,1)} %collective-permute-done.2.refs_3_, ...), custom_call_target="tpu_custom_call" | custom-call | tf_op jit(solution)/shard_map/pallas_call | solution.py:81
  114.4 1.6 copy-done
  116.0 5.0 %all-to-all-start.3 = ((bf16[64,48,512]{2,1,0:T(8,128)(2,1)}), bf16[64,48,512]{2,1,0:T(8,128)(2,1)S(1)}, u32[]{:S(2)}, u32[]{:S(2)}) async-start(bf16[64,48,512]{2,1,0:T(8,128)(2,1)} %bitcast.14), calls=%async_computation.3 | async-start | bytes 6291456 | tf_op jit(solution)/shard_map/all_to_all | solution.py:40
  121.0 1.4 collective-permute-start.14
  122.4 0.1 collective-permute-start.15
  122.5 0.4 collective-permute-start.16
  122.9 3.5 %collective-permute-done.14.gate_b_ref = bf16[2048,512]{1,0:T(8,128)(2,1)S(1)} collective-permute-done((bf16[2048,512]{1,0:T(8,128)(2,1)}, bf16[2048,512]{1,0:T(8,128)(2,1)S(1)}, u32[]{:S(2)}, u32[]{:S(2)}) %collective-permute-start.14) | collective-permute-done | bytes 2097184 | tf_op jit(solution)/shard_map/ppermute | solution.py:30
  126.4 1.3 copy-done.4
  127.7 1.7 collective-permute-done.15.up_b_ref
  129.4 1.3 copy-done.6
  130.7 1.7 collective-permute-done.16.down_b_ref
  132.4 1.4 copy-done.8
  133.8 25.2 %all-to-all-done.3.rows_ref = bf16[64,48,512]{2,1,0:T(8,128)(2,1)S(1)} async-done(((bf16[64,48,512]{2,1,0:T(8,128)(2,1)}), bf16[64,48,512]{2,1,0:T(8,128)(2,1)S(1)}, u32[]{:S(2)}, u32[]{:S(2)}) %all-to-all-start.3) | async-done | bytes 3145760 | tf_op jit(solution)/shard_map/all_to_all | solution.py:40
  159.0 1.6 copy-done.1
  160.6 1.6 copy-done.2
  162.2 1.6 copy-done.3
  163.8 1.6 copy-done.5
  165.4 1.6 copy-done.7
  167.0 1.6 copy-done.9
  168.6 10.9 %shard_map.151 = bf16[64,48,512]{2,1,0:T(8,128)(2,1)S(1)} custom-call(bf16[64,48,512]{2,1,0:T(8,128)(2,1)S(1)} %all-to-all-done.3.rows_ref, bf16[256,256]{1,0:T(8,128)(2,1)S(1)} %copy-done.14, bf16[256,256]{1,0:T(8,128)(2,1)S(1)} %copy-done.15, bf16[2048,512]{1,0:T(8,128)(2,1)S(1)} %bitcast.16, bf16[2048,512]{1,0:T(8,128)(2,1)S(1)} %bitcast.18, ...), custom_call_target="tpu_custom_call" | custom-call | tf_op jit(solution)/shard_map/pallas_call | solution.py:81
  179.5 52.6 %all_to_all.27 = bf16[64,48,512]{2,1,0:T(8,128)(2,1)S(1)} all-to-all(bf16[64,48,512]{2,1,0:T(8,128)(2,1)S(1)} %shard_map.151), channel_id=1, replica_groups=mesh['x'=4,'z'=4,'y'=4,'c'=2] {'x','z','y'}, dimensions={0} | all-to-all | bytes 6291456 | tf_op jit(solution)/shard_map/all_to_all | solution.py:40
  232.1 1.7 shard_map.152
  (34 shorter events, 0.1 us)
Async XLA Ops:
  0.0 25.6 %collective-permute-start = (bf16[256,2048]{1,0:T(8,128)(2,1)}, bf16[256,2048]{1,0:T(8,128)(2,1)S(1)}, u32[]{:S(2)}, u32[]{:S(2)}) collective-permute-start(bf16[256,2048]{1,0:T(8,128)(2,1)} %refs_3_.1), channel_id=1, source_target_pairs={{0,2},{1,7},{2,4},{3,1},{4,6},{5,3},{6,0},{7,5},{8,10},{9,15},{10,... | collective-permute-start | bytes 3145736 | tf_op jit(solution)/shard_map/ppermute | solution.py:36
  3.6 52.8 %collective-permute-start.1 = (bf16[256,2048]{1,0:T(8,128)(2,1)}, bf16[256,2048]{1,0:T(8,128)(2,1)}, u32[]{:S(2)}, u32[]{:S(2)}) collective-permute-start(bf16[256,2048]{1,0:T(8,128)(2,1)} %refs_3_.1), channel_id=1, source_target_pairs={{0,6},{1,3},{2,0},{3,5},{4,2},{5,7},{6,4},{7,1},{8,14},{9,11},{10,... | collective-permute-start | bytes 3145736 | tf_op jit(solution)/shard_map/ppermute | solution.py:36
  25.6 31.3 %collective-permute-start.2 = (bf16[256,2048]{1,0:T(8,128)(2,1)S(1)}, bf16[256,2048]{1,0:T(8,128)(2,1)}, u32[]{:S(2)}, u32[]{:S(2)}) collective-permute-start(bf16[256,2048]{1,0:T(8,128)(2,1)S(1)} %collective-permute-done.refs_1_), channel_id=1, source_target_pairs={{0,2},{1,7},{2,4},{3,1},{4,6},{5,3},{6,0},{7,5},{8,10},{9,15},{10,... | collective-permute-start | bytes 3145736 | tf_op jit(solution)/shard_map/ppermute | solution.py:36
  30.0 16.3 %collective-permute-start.7 = (bf16[512,256]{1,0:T(8,128)(2,1)S(1)}, bf16[512,256]{1,0:T(8,128)(2,1)S(1)}, u32[]{:S(2)}, u32[]{:S(2)}) collective-permute-start(bf16[512,256]{1,0:T(8,128)(2,1)S(1)} %reshape.36.refs_0_), channel_id=1, source_target_pairs={{0,2},{1,7},{2,4},{3,1},{4,6},{5,3},{6,0},{7,5},{8,10},{9,15},{10,... | collective-permute-start | bytes 786440 | tf_op jit(solution)/shard_map/ppermute | solution.py:36
  30.1 19.4 %collective-permute-start.8 = (bf16[512,256]{1,0:T(8,128)(2,1)S(1)}, bf16[512,256]{1,0:T(8,128)(2,1)S(1)}, u32[]{:S(2)}, u32[]{:S(2)}) collective-permute-start(bf16[512,256]{1,0:T(8,128)(2,1)S(1)} %reshape.36.refs_0_), channel_id=1, source_target_pairs={{0,6},{1,3},{2,0},{3,5},{4,2},{5,7},{6,4},{7,1},{8,14},{9,11},{10,... | collective-permute-start | bytes 786440 | tf_op jit(solution)/shard_map/ppermute | solution.py:36
  31.6 17.9 %collective-permute-start.10 = (bf16[512,256]{1,0:T(8,128)(2,1)S(1)}, bf16[512,256]{1,0:T(8,128)(2,1)S(1)}, u32[]{:S(2)}, u32[]{:S(2)}) collective-permute-start(bf16[512,256]{1,0:T(8,128)(2,1)S(1)} %reshape.36.refs_0_), channel_id=1, source_target_pairs={{0,1},{1,0},{2,3},{3,2},{4,5},{5,4},{6,7},{7,6},{8,9},{9,8},{10,11... | collective-permute-start | bytes 786440 | tf_op jit(solution)/shard_map/ppermute | solution.py:30
  46.4 6.4 %collective-permute-start.9 = (bf16[512,256]{1,0:T(8,128)(2,1)S(1)}, bf16[512,256]{1,0:T(8,128)(2,1)S(1)}, u32[]{:S(2)}, u32[]{:S(2)}) collective-permute-start(bf16[512,256]{1,0:T(8,128)(2,1)S(1)} %collective-permute-done.7.refs_1_), channel_id=1, source_target_pairs={{0,2},{1,7},{2,4},{3,1},{4,6},{5,3},{6,0},{7,5},{8,10},{9,15},{10,... | collective-permute-start | bytes 786440 | tf_op jit(solution)/shard_map/ppermute | solution.py:36
  49.5 6.9 %collective-permute-start.11 = (bf16[512,256]{1,0:T(8,128)(2,1)S(1)}, bf16[512,256]{1,0:T(8,128)(2,1)S(1)}, u32[]{:S(2)}, u32[]{:S(2)}) collective-permute-start(bf16[512,256]{1,0:T(8,128)(2,1)S(1)} %collective-permute-done.7.refs_1_), channel_id=1, source_target_pairs={{0,1},{1,0},{2,3},{3,2},{4,5},{5,4},{6,7},{7,6},{8,9},{9,8},{10,11... | collective-permute-start | bytes 786440 | tf_op jit(solution)/shard_map/ppermute | solution.py:30
  49.5 7.4 %collective-permute-start.12 = (bf16[512,256]{1,0:T(8,128)(2,1)S(1)}, bf16[512,256]{1,0:T(8,128)(2,1)S(1)}, u32[]{:S(2)}, u32[]{:S(2)}) collective-permute-start(bf16[512,256]{1,0:T(8,128)(2,1)S(1)} %collective-permute-done.8.refs_2_), channel_id=1, source_target_pairs={{0,1},{1,0},{2,3},{3,2},{4,5},{5,4},{6,7},{7,6},{8,9},{9,8},{10,11... | collective-permute-start | bytes 786440 | tf_op jit(solution)/shard_map/ppermute | solution.py:30
  52.8 48.4 %collective-permute-start.3 = (bf16[256,2048]{1,0:T(8,128)(2,1)}, bf16[256,2048]{1,0:T(8,128)(2,1)}, u32[]{:S(2)}, u32[]{:S(2)}) collective-permute-start(bf16[256,2048]{1,0:T(8,128)(2,1)} %refs_3_.1), channel_id=1, source_target_pairs={{0,1},{1,0},{2,3},{3,2},{4,5},{5,4},{6,7},{7,6},{8,9},{9,8},{10,11... | collective-permute-start | bytes 3145736 | tf_op jit(solution)/shard_map/ppermute | solution.py:30
  56.3 51.4 %collective-permute-start.4 = (bf16[256,2048]{1,0:T(8,128)(2,1)S(1)}, bf16[256,2048]{1,0:T(8,128)(2,1)}, u32[]{:S(2)}, u32[]{:S(2)}) collective-permute-start(bf16[256,2048]{1,0:T(8,128)(2,1)S(1)} %collective-permute-done.refs_1_), channel_id=1, source_target_pairs={{0,1},{1,0},{2,3},{3,2},{4,5},{5,4},{6,7},{7,6},{8,9},{9,8},{10,11... | collective-permute-start | bytes 3145736 | tf_op jit(solution)/shard_map/ppermute | solution.py:30
  56.3 51.3 %collective-permute-start.5 = (bf16[256,2048]{1,0:T(8,128)(2,1)}, bf16[256,2048]{1,0:T(8,128)(2,1)}, u32[]{:S(2)}, u32[]{:S(2)}) collective-permute-start(bf16[256,2048]{1,0:T(8,128)(2,1)} %collective-permute-done.1.refs_2_), channel_id=1, source_target_pairs={{0,1},{1,0},{2,3},{3,2},{4,5},{5,4},{6,7},{7,6},{8,9},{9,8},{10,11... | collective-permute-start | bytes 3145736 | tf_op jit(solution)/shard_map/ppermute | solution.py:30
  56.9 50.8 %collective-permute-start.6 = (bf16[256,2048]{1,0:T(8,128)(2,1)}, bf16[256,2048]{1,0:T(8,128)(2,1)}, u32[]{:S(2)}, u32[]{:S(2)}) collective-permute-start(bf16[256,2048]{1,0:T(8,128)(2,1)} %collective-permute-done.2.refs_3_), channel_id=1, source_target_pairs={{0,1},{1,0},{2,3},{3,2},{4,5},{5,4},{6,7},{7,6},{8,9},{9,8},{10,11... | collective-permute-start | bytes 3145736 | tf_op jit(solution)/shard_map/ppermute | solution.py:30
  56.9 7.2 %collective-permute-start.13 = (bf16[512,256]{1,0:T(8,128)(2,1)S(1)}, bf16[512,256]{1,0:T(8,128)(2,1)S(1)}, u32[]{:S(2)}, u32[]{:S(2)}) collective-permute-start(bf16[512,256]{1,0:T(8,128)(2,1)S(1)} %collective-permute-done.9.refs_3_), channel_id=1, source_target_pairs={{0,1},{1,0},{2,3},{3,2},{4,5},{5,4},{6,7},{7,6},{8,9},{9,8},{10,11... | collective-permute-start | bytes 786440 | tf_op jit(solution)/shard_map/ppermute | solution.py:30
  61.5 1.0 copy-start.11
  95.2 12.5 %all-to-all-start.2 = ((bf16[8,64,256]{2,1,0:T(8,128)(2,1)}), bf16[8,64,256]{2,1,0:T(8,128)(2,1)S(1)}, u32[]{:S(2)}, u32[]{:S(2)}) async-start(bf16[8,64,256]{2,1,0:T(8,128)(2,1)} %bitcast.6), calls=%async_computation.2 | async-start | bytes 524288 | tf_op jit(solution)/shard_map/all_to_all | solution.py:40
  107.7 1.2 copy-start.12
  114.4 1.6 copy-start
  116.0 43.0 %copy-start.14 = (bf16[256,256]{1,0:T(8,128)(2,1)S(1)}, bf16[256,256]{1,0:T(8,128)(2,1)}, u32[]{:S(2)}) copy-start(bf16[256,256]{1,0:T(8,128)(2,1)} %constant.4.clone.order_ref) | copy-start | bytes 393220
  116.0 43.0 %copy-start.15 = (bf16[256,256]{1,0:T(8,128)(2,1)S(1)}, bf16[256,256]{1,0:T(8,128)(2,1)}, u32[]{:S(2)}) copy-start(bf16[256,256]{1,0:T(8,128)(2,1)} %constant.5.clone.back_ref) | copy-start | bytes 393220
  116.0 43.0 %all-to-all-start.3 = ((bf16[64,48,512]{2,1,0:T(8,128)(2,1)}), bf16[64,48,512]{2,1,0:T(8,128)(2,1)S(1)}, u32[]{:S(2)}, u32[]{:S(2)}) async-start(bf16[64,48,512]{2,1,0:T(8,128)(2,1)} %bitcast.14), calls=%async_computation.3 | async-start | bytes 6291456 | tf_op jit(solution)/shard_map/all_to_all | solution.py:40
  121.0 5.4 %collective-permute-start.14 = (bf16[2048,512]{1,0:T(8,128)(2,1)}, bf16[2048,512]{1,0:T(8,128)(2,1)S(1)}, u32[]{:S(2)}, u32[]{:S(2)}) collective-permute-start(bf16[2048,512]{1,0:T(8,128)(2,1)} %bitcast.15), channel_id=1, source_target_pairs={{0,1},{1,0},{2,3},{3,2},{4,5},{5,4},{6,7},{7,6},{8,9},{9,8},{10,11... | collective-permute-start | bytes 6291464 | tf_op jit(solution)/shard_map/ppermute | solution.py:30
  122.4 7.0 %collective-permute-start.15 = (bf16[2048,512]{1,0:T(8,128)(2,1)}, bf16[2048,512]{1,0:T(8,128)(2,1)S(1)}, u32[]{:S(2)}, u32[]{:S(2)}) collective-permute-start(bf16[2048,512]{1,0:T(8,128)(2,1)} %bitcast.17), channel_id=1, source_target_pairs={{0,1},{1,0},{2,3},{3,2},{4,5},{5,4},{6,7},{7,6},{8,9},{9,8},{10,11... | collective-permute-start | bytes 6291464 | tf_op jit(solution)/shard_map/ppermute | solution.py:30
  122.5 9.9 %collective-permute-start.16 = (bf16[512,2048]{1,0:T(8,128)(2,1)}, bf16[512,2048]{1,0:T(8,128)(2,1)S(1)}, u32[]{:S(2)}, u32[]{:S(2)}) collective-permute-start(bf16[512,2048]{1,0:T(8,128)(2,1)} %bitcast.19), channel_id=1, source_target_pairs={{0,1},{1,0},{2,3},{3,2},{4,5},{5,4},{6,7},{7,6},{8,9},{9,8},{10,11... | collective-permute-start | bytes 6291464 | tf_op jit(solution)/shard_map/ppermute | solution.py:30
  126.4 1.3 copy-start.4
  129.4 1.3 copy-start.6
  132.4 1.4 copy-start.8
  159.0 1.6 copy-start.1
  160.6 1.6 copy-start.2
  162.2 1.6 copy-start.3
  163.8 1.6 copy-start.5
  165.4 1.6 copy-start.7
  167.0 1.6 copy-start.9
  179.5 52.6 %copy-start.10 = (bf16[256,3072]{1,0:T(8,128)(2,1)S(1)}, bf16[256,3072]{1,0:T(8,128)(2,1)}, u32[]{:S(2)}) copy-start(bf16[256,3072]{1,0:T(8,128)(2,1)} %get-tuple-element.31.table_ref) | copy-start | bytes 4718596
  179.5 52.6 %copy-start.13 = (f32[64,2048]{1,0:T(8,128)S(1)}, f32[64,2048]{1,0:T(8,128)}, u32[]{:S(2)}) copy-start(f32[64,2048]{1,0:T(8,128)} %get-tuple-element.32.residual_ref) | copy-start | bytes 1572868
where the time goes:
time: 236 us; the launch traced here: 234 us
  blocking collectives  79 us (33%)
  waiting for transfers between devices  76.5 us (32%)
  starting transfers between devices  31.3 us (13%)
  Pallas kernels  28.5 us (12%)
  local copies, waits for them, and re-layouts  18.4 us (8%)
    all_to_all x3, blocking collectives, exchanged(): return lax.all_to_all(x, axes, split_axis=0, concat_axis=0, tiled=True)  79 us
    ppermute x6, waiting for transfers between devices, swirled(): return lax.ppermute(x, ('y', 'c'), pairs)  37.9 us
    all_to_all x2, waiting for transfers between devices, exchanged(): return lax.all_to_all(x, axes, split_axis=0, concat_axis=0, tiled=True)  31.7 us
    pallas_call x8, Pallas kernels, call(): pl.pallas_call(kernel, out_shape=out_shape, in_specs=[x.spec for x in arg...  28.5 us
    unnamed x32, local copies, waits for them, and re-layouts  17.4 us
    ppermute x6, starting transfers between devices, swirled(): return lax.ppermute(x, ('y', 'c'), pairs)  11.6 us
    all_to_all x2, starting transfers between devices, exchanged(): return lax.all_to_all(x, axes, split_axis=0, concat_axis=0, tiled=True)  11 us
    ppermute x11, starting transfers between devices, shifted(): return lax.ppermute(x, axis, [(i, (i + by) % count) for i in range(count)])  8.71 us
  transfers between devices with their start and end apart: 19, of which 8 were waited for; matrix products, arithmetic and copies ran while one was open for 0% of the time, Pallas kernels for 4%

commit v1 on v0

--- a/solution.py
+++ b/solution.py
@@ -16,7 +16,7 @@
 WIDE = 8
 REST = CAP - WIDE
 GROUP = 16
-EARLY = (0, 1, 2, 4)
+EARLY = (0, 1, 4, 5)
 
 norm_eps = 1e-05
 head_eps = 1e-06
@@ -330,7 +330,8 @@
     far = swirled(first, 1)
     pieces = [mine, first, second, far]
     pieces = pieces + [shifted(mine, "c", 1)]
-    pieces = pieces + [shifted(p, "c", 1) for p in (first, second)]
+    pieces = pieces + [shifted(first, "c", 1)]
+    pieces = pieces + [shifted(second, "c", 1)]
     pieces = pieces + [shifted(far, "c", 1)]
 
     out_first = swirled(out_weight, 1)

time: 236 us -> 236 us (level)
  no operation moved by 1% of the time
where the time goes in v1:
time: 236 us; the launch traced here: 233 us
  blocking collectives  78.6 us (33%)
  waiting for transfers between devices  78.2 us (33%)
  starting transfers between devices  29.5 us (12%)
  Pallas kernels  28.5 us (12%)
  local copies, waits for them, and re-layouts  18.4 us (8%)
    all_to_all x3, blocking collectives, exchanged(): return lax.all_to_all(x, axes, split_axis=0, concat_axis=0, tiled=True)  78.6 us
    ppermute x6, waiting for transfers between devices, swirled(): return lax.ppermute(x, ('y', 'c'), pairs)  39.6 us
    all_to_all x2, waiting for transfers between devices, exchanged(): return lax.all_to_all(x, axes, split_axis=0, concat_axis=0, tiled=True)  31.7 us
    pallas_call x8, Pallas kernels, call(): pl.pallas_call(kernel, out_shape=out_shape, in_specs=[x.spec for x in arg...  28.5 us
    unnamed x32, local copies, waits for them, and re-layouts  17.4 us
    all_to_all x2, starting transfers between devices, exchanged(): return lax.all_to_all(x, axes, split_axis=0, concat_axis=0, tiled=True)  11.3 us
    ppermute x6, starting transfers between devices, swirled(): return lax.ppermute(x, ('y', 'c'), pairs)  9.8 us
    ppermute x11, starting transfers between devices, shifted(): return lax.ppermute(x, axis, [(i, (i + by) % count) for i in range(count)])  8.37 us
  transfers between devices with their start and end apart: 19, of which 8 were waited for; matrix products, arithmetic and copies ran while one was open for 0% of the time, Pallas kernels for 4%

profile of v1, /device:TPU:1, one launch (start us, length us, event | category | flops | bytes accessed | tf_op | source)
XLA Modules:
  0.0 233.3 jit_solution(292196134581222929)
XLA Ops:
  0.0 3.6 %collective-permute-start = (bf16[256,2048]{1,0:T(8,128)(2,1)}, bf16[256,2048]{1,0:T(8,128)(2,1)S(1)}, u32[]{:S(2)}, u32[]{:S(2)}) collective-permute-start(bf16[256,2048]{1,0:T(8,128)(2,1)} %refs_3_.1), channel_id=1, source_target_pairs={{0,2},{1,7},{2,4},{3,1},{4,6},{5,3},{6,0},{7,5},{8,10},{9,15},{10,... | collective-permute-start | bytes 3145736 | tf_op jit(solution)/shard_map/ppermute | solution.py:36
  3.6 22.0 %collective-permute-done.refs_1_ = bf16[256,2048]{1,0:T(8,128)(2,1)S(1)} collective-permute-done((bf16[256,2048]{1,0:T(8,128)(2,1)}, bf16[256,2048]{1,0:T(8,128)(2,1)S(1)}, u32[]{:S(2)}, u32[]{:S(2)}) %collective-permute-start) | collective-permute-done | bytes 1048608 | tf_op jit(solution)/shard_map/ppermute | solution.py:36
  25.6 3.4 %collective-permute-start.2 = (bf16[256,2048]{1,0:T(8,128)(2,1)S(1)}, bf16[256,2048]{1,0:T(8,128)(2,1)}, u32[]{:S(2)}, u32[]{:S(2)}) collective-permute-start(bf16[256,2048]{1,0:T(8,128)(2,1)S(1)} %collective-permute-done.refs_1_), channel_id=1, source_target_pairs={{0,2},{1,7},{2,4},{3,1},{4,6},{5,3},{6,0},{7,5},{8,10},{9,15},{10,... | collective-permute-start | bytes 3145736 | tf_op jit(solution)/shard_map/ppermute | solution.py:36
  29.0 1.0 reshape.36.refs_0_
  30.0 0.1 collective-permute-start.7
  30.1 0.9 collective-permute-start.10
  31.0 1.3 collective-permute-start.8
  32.3 14.1 %collective-permute-done.7.refs_1_ = bf16[512,256]{1,0:T(8,128)(2,1)S(1)} collective-permute-done((bf16[512,256]{1,0:T(8,128)(2,1)S(1)}, bf16[512,256]{1,0:T(8,128)(2,1)S(1)}, u32[]{:S(2)}, u32[]{:S(2)}) %collective-permute-start.7) | collective-permute-done | bytes 262176 | tf_op jit(solution)/shard_map/ppermute | solution.py:36
  46.4 2.4 %collective-permute-start.11 = (bf16[512,256]{1,0:T(8,128)(2,1)S(1)}, bf16[512,256]{1,0:T(8,128)(2,1)S(1)}, u32[]{:S(2)}, u32[]{:S(2)}) collective-permute-start(bf16[512,256]{1,0:T(8,128)(2,1)S(1)} %collective-permute-done.7.refs_1_), channel_id=1, source_target_pairs={{0,1},{1,0},{2,3},{3,2},{4,5},{5,4},{6,7},{7,6},{8,9},{9,8},{10,11... | collective-permute-start | bytes 786440 | tf_op jit(solution)/shard_map/ppermute | solution.py:30
  48.8 1.5 collective-permute-start.9
  50.2 0.5 collective-permute-start.3
  50.7 3.5 %collective-permute-done.9.refs_3_ = bf16[512,256]{1,0:T(8,128)(2,1)S(1)} collective-permute-done((bf16[512,256]{1,0:T(8,128)(2,1)S(1)}, bf16[512,256]{1,0:T(8,128)(2,1)S(1)}, u32[]{:S(2)}, u32[]{:S(2)}) %collective-permute-start.9) | collective-permute-done | bytes 262176 | tf_op jit(solution)/shard_map/ppermute | solution.py:36
  54.3 2.1 collective-permute-start.4
  56.3 0.0 collective-permute-start.5
  56.4 0.5 collective-permute-start.6
  56.9 0.1 collective-permute-start.13
  57.0 4.1 %shard_map.145 = (bf16[3072,256]{1,0:T(8,128)(2,1)S(1)}, bf16[256,3072]{1,0:T(8,128)(2,1)}, bf16[2048,256]{1,0:T(8,128)(2,1)S(1)}, bf16[2048,256]{1,0:T(8,128)(2...) custom-call(s32[4,8,16]{2,1,0:T(8,128)} %bitcast.23, f32[4,8,16]{2,1,0:T(8,128)} %bitcast.24, ...), custom_call_target="tpu_custom_call" | custom-call | tf_op jit(solution)/shard_map/pallas_call | solution.py:81
  61.1 1.0 copy-done.11
  62.0 1.7 shard_map.146
  63.7 2.7 %shard_map.147 = (bf16[512,256]{1,0:T(8,128)(2,1)S(1)}, f32[512,256]{1,0:T(8,128)S(1)}, bf16[1024,128]{1,0:T(8,128)(2,1)S(1)}, bf16[64,2048]{1,0:T(8,128)(2,1)S(1)}) custom-call(bf16[512,256]{1,0:T(8,128)(2,1)S(1)} %reshape.36.refs_0_, bf16[512,256]{1,0:T(8,128)(2,1)S(1)} %collective-permute-done.7.refs_1_, ...), custom_call_target="tpu_custom_call" | custom-call | tf_op jit(solution)/shard_map/pallas_call | solution.py:81
  66.5 15.2 %all_to_all.25.states_ref = bf16[16,64,128]{2,1,0:T(8,128)(2,1)S(1)} all-to-all(bf16[16,64,128]{2,1,0:T(8,128)(2,1)S(1)} %bitcast.22), channel_id=1, replica_groups=mesh['x'=4,'z'=4,'y'=4,'c'=2] {'x','z'}, dimensions={0} | all-to-all | bytes 524288 | tf_op jit(solution)/shard_map/all_to_all | solution.py:40
  81.7 10.8 %all_to_all.26 = bf16[16,64,128]{2,1,0:T(8,128)(2,1)S(1)} all-to-all(bf16[16,64,128]{2,1,0:T(8,128)(2,1)S(1)} %shard_map.148), channel_id=1, replica_groups=mesh['x'=4,'z'=4,'y'=4,'c'=2] {'x','z'}, dimensions={0} | all-to-all | bytes 524288 | tf_op jit(solution)/shard_map/all_to_all | solution.py:40
  92.5 1.9 shard_map.149
  94.4 6.3 %all-to-all-start.2 = ((bf16[8,64,256]{2,1,0:T(8,128)(2,1)}), bf16[8,64,256]{2,1,0:T(8,128)(2,1)S(1)}, u32[]{:S(2)}, u32[]{:S(2)}) async-start(bf16[8,64,256]{2,1,0:T(8,128)(2,1)} %bitcast.6), calls=%async_computation.2 | async-start | bytes 524288 | tf_op jit(solution)/shard_map/all_to_all | solution.py:40
  100.7 6.5 %all-to-all-done.2.refs_8_ = bf16[8,64,256]{2,1,0:T(8,128)(2,1)S(1)} async-done(((bf16[8,64,256]{2,1,0:T(8,128)(2,1)}), bf16[8,64,256]{2,1,0:T(8,128)(2,1)S(1)}, u32[]{:S(2)}, u32[]{:S(2)}) %all-to-all-start.2) | async-done | bytes 262176 | tf_op jit(solution)/shard_map/all_to_all | solution.py:40
  107.2 1.2 copy-done.12
  108.4 5.5 %shard_map.150 = (f32[64,2048]{1,0:T(8,128)}, bf16[3072,512]{1,0:T(8,128)(2,1)S(1)}) custom-call(bf16[256,2048]{1,0:T(8,128)(2,1)S(1)} %copy-done.12, bf16[256,2048]{1,0:T(8,128)(2,1)S(1)} %collective-permute-done.refs_1_, bf16[256,2048]{1,0:T(8,128)(2,1)} %collective-permute-done.1.refs_2_, bf16[256,2048]{1,0:T(8,128)(2,1)} %collective-permute-done.2.refs_3_, ...), custom_call_target="tpu_custom_call" | custom-call | tf_op jit(solution)/shard_map/pallas_call | solution.py:81
  113.9 1.6 copy-done
  115.5 5.0 %all-to-all-start.3 = ((bf16[64,48,512]{2,1,0:T(8,128)(2,1)}), bf16[64,48,512]{2,1,0:T(8,128)(2,1)S(1)}, u32[]{:S(2)}, u32[]{:S(2)}) async-start(bf16[64,48,512]{2,1,0:T(8,128)(2,1)} %bitcast.14), calls=%async_computation.3 | async-start | bytes 6291456 | tf_op jit(solution)/shard_map/all_to_all | solution.py:40
  120.6 1.4 collective-permute-start.14
  122.0 0.1 collective-permute-start.15
  122.1 0.4 collective-permute-start.16
  122.5 3.5 %collective-permute-done.14.gate_b_ref = bf16[2048,512]{1,0:T(8,128)(2,1)S(1)} collective-permute-done((bf16[2048,512]{1,0:T(8,128)(2,1)}, bf16[2048,512]{1,0:T(8,128)(2,1)S(1)}, u32[]{:S(2)}, u32[]{:S(2)}) %collective-permute-start.14) | collective-permute-done | bytes 2097184 | tf_op jit(solution)/shard_map/ppermute | solution.py:30
  126.0 1.3 copy-done.4
  127.3 1.7 collective-permute-done.15.up_b_ref
  129.0 1.3 copy-done.6
  130.3 1.7 collective-permute-done.16.down_b_ref
  132.0 1.4 copy-done.8
  133.3 25.2 %all-to-all-done.3.rows_ref = bf16[64,48,512]{2,1,0:T(8,128)(2,1)S(1)} async-done(((bf16[64,48,512]{2,1,0:T(8,128)(2,1)}), bf16[64,48,512]{2,1,0:T(8,128)(2,1)S(1)}, u32[]{:S(2)}, u32[]{:S(2)}) %all-to-all-start.3) | async-done | bytes 3145760 | tf_op jit(solution)/shard_map/all_to_all | solution.py:40
  158.6 1.6 copy-done.1
  160.2 1.6 copy-done.2
  161.8 1.6 copy-done.3
  163.4 1.6 copy-done.5
  164.9 1.6 copy-done.7
  166.5 1.6 copy-done.9
  168.1 10.9 %shard_map.151 = bf16[64,48,512]{2,1,0:T(8,128)(2,1)S(1)} custom-call(bf16[64,48,512]{2,1,0:T(8,128)(2,1)S(1)} %all-to-all-done.3.rows_ref, bf16[256,256]{1,0:T(8,128)(2,1)S(1)} %copy-done.14, bf16[256,256]{1,0:T(8,128)(2,1)S(1)} %copy-done.15, bf16[2048,512]{1,0:T(8,128)(2,1)S(1)} %bitcast.16, bf16[2048,512]{1,0:T(8,128)(2,1)S(1)} %bitcast.18, ...), custom_call_target="tpu_custom_call" | custom-call | tf_op jit(solution)/shard_map/pallas_call | solution.py:81
  179.0 52.6 %all_to_all.27 = bf16[64,48,512]{2,1,0:T(8,128)(2,1)S(1)} all-to-all(bf16[64,48,512]{2,1,0:T(8,128)(2,1)S(1)} %shard_map.151), channel_id=1, replica_groups=mesh['x'=4,'z'=4,'y'=4,'c'=2] {'x','z','y'}, dimensions={0} | all-to-all | bytes 6291456 | tf_op jit(solution)/shard_map/all_to_all | solution.py:40
  231.6 1.7 shard_map.152
  (34 shorter events, 0.1 us)
Async XLA Ops:
  0.0 25.6 %collective-permute-start = (bf16[256,2048]{1,0:T(8,128)(2,1)}, bf16[256,2048]{1,0:T(8,128)(2,1)S(1)}, u32[]{:S(2)}, u32[]{:S(2)}) collective-permute-start(bf16[256,2048]{1,0:T(8,128)(2,1)} %refs_3_.1), channel_id=1, source_target_pairs={{0,2},{1,7},{2,4},{3,1},{4,6},{5,3},{6,0},{7,5},{8,10},{9,15},{10,... | collective-permute-start | bytes 3145736 | tf_op jit(solution)/shard_map/ppermute | solution.py:36
  3.6 52.8 %collective-permute-start.1 = (bf16[256,2048]{1,0:T(8,128)(2,1)}, bf16[256,2048]{1,0:T(8,128)(2,1)}, u32[]{:S(2)}, u32[]{:S(2)}) collective-permute-start(bf16[256,2048]{1,0:T(8,128)(2,1)} %refs_3_.1), channel_id=1, source_target_pairs={{0,6},{1,3},{2,0},{3,5},{4,2},{5,7},{6,4},{7,1},{8,14},{9,11},{10,... | collective-permute-start | bytes 3145736 | tf_op jit(solution)/shard_map/ppermute | solution.py:36
  25.6 30.8 %collective-permute-start.2 = (bf16[256,2048]{1,0:T(8,128)(2,1)S(1)}, bf16[256,2048]{1,0:T(8,128)(2,1)}, u32[]{:S(2)}, u32[]{:S(2)}) collective-permute-start(bf16[256,2048]{1,0:T(8,128)(2,1)S(1)} %collective-permute-done.refs_1_), channel_id=1, source_target_pairs={{0,2},{1,7},{2,4},{3,1},{4,6},{5,3},{6,0},{7,5},{8,10},{9,15},{10,... | collective-permute-start | bytes 3145736 | tf_op jit(solution)/shard_map/ppermute | solution.py:36
  30.0 16.3 %collective-permute-start.7 = (bf16[512,256]{1,0:T(8,128)(2,1)S(1)}, bf16[512,256]{1,0:T(8,128)(2,1)S(1)}, u32[]{:S(2)}, u32[]{:S(2)}) collective-permute-start(bf16[512,256]{1,0:T(8,128)(2,1)S(1)} %reshape.36.refs_0_), channel_id=1, source_target_pairs={{0,2},{1,7},{2,4},{3,1},{4,6},{5,3},{6,0},{7,5},{8,10},{9,15},{10,... | collective-permute-start | bytes 786440 | tf_op jit(solution)/shard_map/ppermute | solution.py:36
  30.1 18.6 %collective-permute-start.10 = (bf16[512,256]{1,0:T(8,128)(2,1)S(1)}, bf16[512,256]{1,0:T(8,128)(2,1)S(1)}, u32[]{:S(2)}, u32[]{:S(2)}) collective-permute-start(bf16[512,256]{1,0:T(8,128)(2,1)S(1)} %reshape.36.refs_0_), channel_id=1, source_target_pairs={{0,1},{1,0},{2,3},{3,2},{4,5},{5,4},{6,7},{7,6},{8,9},{9,8},{10,11... | collective-permute-start | bytes 786440 | tf_op jit(solution)/shard_map/ppermute | solution.py:30
  31.0 19.2 %collective-permute-start.8 = (bf16[512,256]{1,0:T(8,128)(2,1)S(1)}, bf16[512,256]{1,0:T(8,128)(2,1)S(1)}, u32[]{:S(2)}, u32[]{:S(2)}) collective-permute-start(bf16[512,256]{1,0:T(8,128)(2,1)S(1)} %reshape.36.refs_0_), channel_id=1, source_target_pairs={{0,6},{1,3},{2,0},{3,5},{4,2},{5,7},{6,4},{7,1},{8,14},{9,11},{10,... | collective-permute-start | bytes 786440 | tf_op jit(solution)/shard_map/ppermute | solution.py:36
  46.4 3.9 %collective-permute-start.11 = (bf16[512,256]{1,0:T(8,128)(2,1)S(1)}, bf16[512,256]{1,0:T(8,128)(2,1)S(1)}, u32[]{:S(2)}, u32[]{:S(2)}) collective-permute-start(bf16[512,256]{1,0:T(8,128)(2,1)S(1)} %collective-permute-done.7.refs_1_), channel_id=1, source_target_pairs={{0,1},{1,0},{2,3},{3,2},{4,5},{5,4},{6,7},{7,6},{8,9},{9,8},{10,11... | collective-permute-start | bytes 786440 | tf_op jit(solution)/shard_map/ppermute | solution.py:30
  48.8 5.5 %collective-permute-start.9 = (bf16[512,256]{1,0:T(8,128)(2,1)S(1)}, bf16[512,256]{1,0:T(8,128)(2,1)S(1)}, u32[]{:S(2)}, u32[]{:S(2)}) collective-permute-start(bf16[512,256]{1,0:T(8,128)(2,1)S(1)} %collective-permute-done.7.refs_1_), channel_id=1, source_target_pairs={{0,2},{1,7},{2,4},{3,1},{4,6},{5,3},{6,0},{7,5},{8,10},{9,15},{10,... | collective-permute-start | bytes 786440 | tf_op jit(solution)/shard_map/ppermute | solution.py:36
  50.2 6.6 %collective-permute-start.12 = (bf16[512,256]{1,0:T(8,128)(2,1)S(1)}, bf16[512,256]{1,0:T(8,128)(2,1)S(1)}, u32[]{:S(2)}, u32[]{:S(2)}) collective-permute-start(bf16[512,256]{1,0:T(8,128)(2,1)S(1)} %collective-permute-done.8.refs_2_), channel_id=1, source_target_pairs={{0,1},{1,0},{2,3},{3,2},{4,5},{5,4},{6,7},{7,6},{8,9},{9,8},{10,11... | collective-permute-start | bytes 786440 | tf_op jit(solution)/shard_map/ppermute | solution.py:30
  50.2 50.5 %collective-permute-start.3 = (bf16[256,2048]{1,0:T(8,128)(2,1)}, bf16[256,2048]{1,0:T(8,128)(2,1)}, u32[]{:S(2)}, u32[]{:S(2)}) collective-permute-start(bf16[256,2048]{1,0:T(8,128)(2,1)} %refs_3_.1), channel_id=1, source_target_pairs={{0,1},{1,0},{2,3},{3,2},{4,5},{5,4},{6,7},{7,6},{8,9},{9,8},{10,11... | collective-permute-start | bytes 3145736 | tf_op jit(solution)/shard_map/ppermute | solution.py:30
  54.3 52.9 %collective-permute-start.4 = (bf16[256,2048]{1,0:T(8,128)(2,1)S(1)}, bf16[256,2048]{1,0:T(8,128)(2,1)}, u32[]{:S(2)}, u32[]{:S(2)}) collective-permute-start(bf16[256,2048]{1,0:T(8,128)(2,1)S(1)} %collective-permute-done.refs_1_), channel_id=1, source_target_pairs={{0,1},{1,0},{2,3},{3,2},{4,5},{5,4},{6,7},{7,6},{8,9},{9,8},{10,11... | collective-permute-start | bytes 3145736 | tf_op jit(solution)/shard_map/ppermute | solution.py:30
  56.3 50.9 %collective-permute-start.5 = (bf16[256,2048]{1,0:T(8,128)(2,1)}, bf16[256,2048]{1,0:T(8,128)(2,1)}, u32[]{:S(2)}, u32[]{:S(2)}) collective-permute-start(bf16[256,2048]{1,0:T(8,128)(2,1)} %collective-permute-done.1.refs_2_), channel_id=1, source_target_pairs={{0,1},{1,0},{2,3},{3,2},{4,5},{5,4},{6,7},{7,6},{8,9},{9,8},{10,11... | collective-permute-start | bytes 3145736 | tf_op jit(solution)/shard_map/ppermute | solution.py:30
  56.4 50.8 %collective-permute-start.6 = (bf16[256,2048]{1,0:T(8,128)(2,1)}, bf16[256,2048]{1,0:T(8,128)(2,1)}, u32[]{:S(2)}, u32[]{:S(2)}) collective-permute-start(bf16[256,2048]{1,0:T(8,128)(2,1)} %collective-permute-done.2.refs_3_), channel_id=1, source_target_pairs={{0,1},{1,0},{2,3},{3,2},{4,5},{5,4},{6,7},{7,6},{8,9},{9,8},{10,11... | collective-permute-start | bytes 3145736 | tf_op jit(solution)/shard_map/ppermute | solution.py:30
  56.9 6.8 %collective-permute-start.13 = (bf16[512,256]{1,0:T(8,128)(2,1)S(1)}, bf16[512,256]{1,0:T(8,128)(2,1)S(1)}, u32[]{:S(2)}, u32[]{:S(2)}) collective-permute-start(bf16[512,256]{1,0:T(8,128)(2,1)S(1)} %collective-permute-done.9.refs_3_), channel_id=1, source_target_pairs={{0,1},{1,0},{2,3},{3,2},{4,5},{5,4},{6,7},{7,6},{8,9},{9,8},{10,11... | collective-permute-start | bytes 786440 | tf_op jit(solution)/shard_map/ppermute | solution.py:30
  61.0 1.0 copy-start.11
  94.4 12.8 %all-to-all-start.2 = ((bf16[8,64,256]{2,1,0:T(8,128)(2,1)}), bf16[8,64,256]{2,1,0:T(8,128)(2,1)S(1)}, u32[]{:S(2)}, u32[]{:S(2)}) async-start(bf16[8,64,256]{2,1,0:T(8,128)(2,1)} %bitcast.6), calls=%async_computation.2 | async-start | bytes 524288 | tf_op jit(solution)/shard_map/all_to_all | solution.py:40
  107.2 1.2 copy-start.12
  113.9 1.6 copy-start
  115.5 43.0 %copy-start.14 = (bf16[256,256]{1,0:T(8,128)(2,1)S(1)}, bf16[256,256]{1,0:T(8,128)(2,1)}, u32[]{:S(2)}) copy-start(bf16[256,256]{1,0:T(8,128)(2,1)} %constant.4.clone.order_ref) | copy-start | bytes 393220
  115.5 43.0 %copy-start.15 = (bf16[256,256]{1,0:T(8,128)(2,1)S(1)}, bf16[256,256]{1,0:T(8,128)(2,1)}, u32[]{:S(2)}) copy-start(bf16[256,256]{1,0:T(8,128)(2,1)} %constant.5.clone.back_ref) | copy-start | bytes 393220
  115.5 43.0 %all-to-all-start.3 = ((bf16[64,48,512]{2,1,0:T(8,128)(2,1)}), bf16[64,48,512]{2,1,0:T(8,128)(2,1)S(1)}, u32[]{:S(2)}, u32[]{:S(2)}) async-start(bf16[64,48,512]{2,1,0:T(8,128)(2,1)} %bitcast.14), calls=%async_computation.3 | async-start | bytes 6291456 | tf_op jit(solution)/shard_map/all_to_all | solution.py:40
  120.6 5.4 %collective-permute-start.14 = (bf16[2048,512]{1,0:T(8,128)(2,1)}, bf16[2048,512]{1,0:T(8,128)(2,1)S(1)}, u32[]{:S(2)}, u32[]{:S(2)}) collective-permute-start(bf16[2048,512]{1,0:T(8,128)(2,1)} %bitcast.15), channel_id=1, source_target_pairs={{0,1},{1,0},{2,3},{3,2},{4,5},{5,4},{6,7},{7,6},{8,9},{9,8},{10,11... | collective-permute-start | bytes 6291464 | tf_op jit(solution)/shard_map/ppermute | solution.py:30
  122.0 7.0 %collective-permute-start.15 = (bf16[2048,512]{1,0:T(8,128)(2,1)}, bf16[2048,512]{1,0:T(8,128)(2,1)S(1)}, u32[]{:S(2)}, u32[]{:S(2)}) collective-permute-start(bf16[2048,512]{1,0:T(8,128)(2,1)} %bitcast.17), channel_id=1, source_target_pairs={{0,1},{1,0},{2,3},{3,2},{4,5},{5,4},{6,7},{7,6},{8,9},{9,8},{10,11... | collective-permute-start | bytes 6291464 | tf_op jit(solution)/shard_map/ppermute | solution.py:30
  122.1 9.9 %collective-permute-start.16 = (bf16[512,2048]{1,0:T(8,128)(2,1)}, bf16[512,2048]{1,0:T(8,128)(2,1)S(1)}, u32[]{:S(2)}, u32[]{:S(2)}) collective-permute-start(bf16[512,2048]{1,0:T(8,128)(2,1)} %bitcast.19), channel_id=1, source_target_pairs={{0,1},{1,0},{2,3},{3,2},{4,5},{5,4},{6,7},{7,6},{8,9},{9,8},{10,11... | collective-permute-start | bytes 6291464 | tf_op jit(solution)/shard_map/ppermute | solution.py:30
  126.0 1.3 copy-start.4
  129.0 1.3 copy-start.6
  132.0 1.4 copy-start.8
  158.6 1.6 copy-start.1
  160.2 1.6 copy-start.2
  161.8 1.6 copy-start.3
  163.3 1.6 copy-start.5
  164.9 1.6 copy-start.7
  166.5 1.6 copy-start.9
  179.0 52.6 %copy-start.10 = (bf16[256,3072]{1,0:T(8,128)(2,1)S(1)}, bf16[256,3072]{1,0:T(8,128)(2,1)}, u32[]{:S(2)}) copy-start(bf16[256,3072]{1,0:T(8,128)(2,1)} %get-tuple-element.31.table_ref) | copy-start | bytes 4718596
  179.0 52.6 %copy-start.13 = (f32[64,2048]{1,0:T(8,128)S(1)}, f32[64,2048]{1,0:T(8,128)}, u32[]{:S(2)}) copy-start(f32[64,2048]{1,0:T(8,128)} %get-tuple-element.32.residual_ref) | copy-start | bytes 1572868
